TPU v7x, 32 devices: a whole 2x2x4 slice. The times are simulated.
32 devices in a mesh: tm: 4 (over x, core), vox: 8 (over z, y).
Axes of the slice: x: 2, y: 2, z: 4, core: 2. Of those that a mesh axis runs over, the one named last changes fastest.
Arguments:
- clip_features: bfloat16 [1024, 1024], P('tm'), may hold values from -6 to 6
- depth_kernel: float32 [3, 1024], replicated, may hold values from -3.5 to 3.5
- point_weight: bfloat16 [1024, 1024], replicated, may hold values from -0.1875 to 0.1875
- session_lengths: int32 [8], replicated, may hold values from 1 to 256, 1024 in all
- subject_feature_gains: float32 [16, 1024], replicated, may hold values from 0.25 to 1.75
- readout_weight: bfloat16 [1024, 5120], P(None, 'vox'), may hold values from -0.1875 to 0.1875
- hrf_kernel: float32 [16, 5120], P(None, 'vox'), may hold values from -1.5 to 1.5
- block_subject: int32 [40], P('vox'), may hold values from 0 to 15, as said below
- block_live: int32 [40], P('vox'), may hold values from 0 to 128, as said below
- bold_target: bfloat16 [1024, 5120], P('tm', 'vox'), may hold values from -6 to 6
Outputs:
- loss_total: float32 [], replicated
- grad_readout: float32 [1024, 5120], P('tm', 'vox')
- grad_point: float32 [1024, 1024], P(None, 'vox')
Inputs may be any that keep to these rules, and one draw needn't show every extreme that they name: `session_lengths`: the lengths sum to 1024; one session has exactly 256 TRs. `block_subject`: ids never fall along the blocks; every subject owns one or two consecutive blocks, subject 0 two; the blocks after the last subject's live ones carry id 16 - 1 and no live voxels. `block_live`: the live voxels of a block are its first slots; a subject's blocks are full except its last, which holds at least one live voxel; blocks after the subjects' blocks are empty.
All inputs are finite; a program needn't handle non-finite values.
Results may differ from a plain program's by a relative error of at most 0.0044.
Values may be sent and summed in bfloat16 or wider, within the bound.
No kernel may reach another device: no remote copies, remote signals or barrier semaphores. Data moves between devices by JAX's collectives and lax.ppermute only.
A program may use at most 64 MiB of HBM per device.

v0:
```python
import jax
import jax.numpy as jnp
from jax import lax
from jax.sharding import PartitionSpec as P

BLOCK_VOX = 128
KERNEL_TAPS = 3
TAP_SPACING = 8
HRF = 16


def from_behind(value, axis, steps):
    count = lax.axis_size(axis)
    first, last = (max(0, -steps), min(count, count - steps))
    return lax.ppermute(value, axis, [(source, source + steps) for source in range(first, last)])


def session_of(session_ends, position):
    return jnp.sum((session_ends[None, :] <= position[:, None]).astype(jnp.int32), axis=1)


def live_block(operands):
    return jnp.dot(operands[0], operands[1], preferred_element_type=jnp.float32).astype(
        jnp.bfloat16
    )


def dead_block(operands):
    return jnp.zeros((operands[0].shape[0], operands[1].shape[1]), jnp.bfloat16)


def shards(
    clip_features,
    depth_kernel,
    point_weight,
    session_lengths,
    subject_feature_gains,
    readout_weight,
    hrf_kernel,
    block_subject,
    block_live,
    bold_target,
):
    local_rows = clip_features.shape[0]
    feature_count = clip_features.shape[1]
    slot_count = readout_weight.shape[1]
    block_count = slot_count // BLOCK_VOX
    subjects = subject_feature_gains.shape[0]
    total_rows = local_rows * lax.axis_size("tm")
    first_row = lax.axis_index("tm") * local_rows
    core_margin_rows = (KERNEL_TAPS - 1) * TAP_SPACING
    filter_rim = HRF - 1
    session_ends = jnp.cumsum(session_lengths)
    earlier = from_behind(clip_features[local_rows - core_margin_rows :], "tm", 1)
    extended = jnp.concatenate([earlier, clip_features], axis=0)
    ext_position = (
        first_row - core_margin_rows + jnp.arange(core_margin_rows + local_rows, dtype=jnp.int32)
    )
    ext_session = session_of(session_ends, ext_position)
    out_rows = core_margin_rows + local_rows - core_margin_rows
    out_session = ext_session[core_margin_rows:]
    depth_sum = jnp.zeros((out_rows, feature_count), jnp.float32)
    for kernel_tap_index in range(KERNEL_TAPS):
        shift_amount = core_margin_rows - kernel_tap_index * TAP_SPACING
        source = extended[shift_amount : shift_amount + out_rows].astype(jnp.float32)
        valid_tap = (ext_position[shift_amount : shift_amount + out_rows] >= 0) & (
            ext_session[shift_amount : shift_amount + out_rows] == out_session
        )
        depth_sum = depth_sum + depth_kernel[kernel_tap_index][None, :] * jnp.where(
            valid_tap[:, None], source, 0.0
        )
    depth_half = depth_sum.astype(jnp.bfloat16)
    pre_act = jnp.dot(depth_half, point_weight, preferred_element_type=jnp.float32)
    core_out = (extended[core_margin_rows:].astype(jnp.float32) + jax.nn.gelu(pre_act)).astype(
        jnp.bfloat16
    )
    one_hot = (block_subject[:, None] == jnp.arange(subjects, dtype=jnp.int32)[None, :]).astype(
        jnp.float32
    )
    gain_rows = jnp.dot(one_hot, subject_feature_gains, precision=lax.Precision.HIGHEST)
    scale_cols = jnp.transpose(gain_rows)[:, :, None]
    effective = (
        (
            readout_weight.astype(jnp.float32).reshape(feature_count, block_count, BLOCK_VOX)
            * scale_cols
        )
        .reshape(feature_count, slot_count)
        .astype(jnp.bfloat16)
    )
    pieces = []
    for block_index in range(block_count):
        weight_cols = effective[:, block_index * BLOCK_VOX : (block_index + 1) * BLOCK_VOX]
        pieces.append(
            lax.cond(block_live[block_index] > 0, live_block, dead_block, (core_out, weight_cols))
        )
    response = jnp.concatenate(pieces, axis=1)
    response_before = from_behind(response[local_rows - filter_rim :], "tm", 1)
    response_ext = jnp.concatenate([response_before, response], axis=0)
    filter_position = first_row - filter_rim + jnp.arange(filter_rim + local_rows, dtype=jnp.int32)
    filter_session = session_of(session_ends, filter_position)
    own_session = filter_session[filter_rim:]
    predicted = jnp.zeros((local_rows, slot_count), jnp.float32)
    for kernel_tap_index in range(HRF):
        shift_amount = filter_rim - kernel_tap_index
        source = response_ext[shift_amount : shift_amount + local_rows].astype(jnp.float32)
        valid_tap = (filter_position[shift_amount : shift_amount + local_rows] >= 0) & (
            filter_session[shift_amount : shift_amount + local_rows] == own_session
        )
        predicted = predicted + hrf_kernel[kernel_tap_index][None, :] * jnp.where(
            valid_tap[:, None], source, 0.0
        )
    local_counts = jnp.dot(block_live.astype(jnp.float32), one_hot, precision=lax.Precision.HIGHEST)
    subject_voxels = lax.psum(local_counts, "vox")
    block_voxels = jnp.dot(one_hot, subject_voxels, precision=lax.Precision.HIGHEST)
    live_mask = (
        (jnp.arange(BLOCK_VOX, dtype=jnp.int32)[None, :] < block_live[:, None])
        .astype(jnp.float32)
        .reshape(slot_count)
    )
    voxel_weight = live_mask / jnp.repeat(block_voxels, BLOCK_VOX)
    misfit = predicted - bold_target.astype(jnp.float32)
    partial_loss = jnp.sum(voxel_weight[None, :] * misfit * misfit)
    loss_total = lax.psum(partial_loss, ("tm", "vox")) / (subjects * total_rows)
    pred_grad = 2.0 * voxel_weight[None, :] * misfit
    later = from_behind(pred_grad[:filter_rim], "tm", -1)
    grad_ext = jnp.concatenate([pred_grad, later], axis=0)
    later_position = first_row + jnp.arange(local_rows + filter_rim, dtype=jnp.int32)
    later_session = session_of(session_ends, later_position)
    response_grad = jnp.zeros((local_rows, slot_count), jnp.float32)
    for kernel_tap_index in range(HRF):
        source = grad_ext[kernel_tap_index : kernel_tap_index + local_rows]
        valid_tap = (
            later_position[kernel_tap_index : kernel_tap_index + local_rows] < total_rows
        ) & (later_session[kernel_tap_index : kernel_tap_index + local_rows] == own_session)
        response_grad = response_grad + hrf_kernel[kernel_tap_index][None, :] * jnp.where(
            valid_tap[:, None], source, 0.0
        )
    response_half = response_grad.astype(jnp.bfloat16)
    raw_rows = lax.dot_general(
        core_out, response_half, (((0,), (0,)), ((), ())), preferred_element_type=jnp.float32
    )
    grad_readout = lax.psum_scatter(
        (
            raw_rows.reshape(
                lax.axis_size("tm") * (feature_count // lax.axis_size("tm")), block_count, BLOCK_VOX
            )
            * jnp.transpose(gain_rows)[:, :, None]
        ).reshape(lax.axis_size("tm") * (feature_count // lax.axis_size("tm")), slot_count),
        "tm",
        scatter_dimension=0,
        tiled=True,
    )
    share_width = feature_count // lax.axis_size("vox")
    col_start = lax.axis_index("vox") * share_width
    pre_cols = lax.dynamic_slice_in_dim(pre_act, col_start, share_width, 1)
    full_grad = lax.dot_general(
        response_half, effective, (((1,), (1,)), ((), ())), preferred_element_type=jnp.float32
    )
    summed_grad = lax.psum(full_grad, "vox")
    grad_cols = lax.dynamic_slice_in_dim(summed_grad, col_start, share_width, 1)
    pre_grad = jax.vjp(jax.nn.gelu, pre_cols)[1](grad_cols)[0].astype(jnp.bfloat16)
    point_part = lax.dot_general(
        depth_half, pre_grad, (((0,), (0,)), ((), ())), preferred_element_type=jnp.float32
    )
    grad_point = lax.psum(point_part, "tm")
    return (loss_total, grad_readout, grad_point)


def solution(mesh):
    placed = (
        P("tm", None),
        P(),
        P(),
        P(),
        P(),
        P(None, "vox"),
        P(None, "vox"),
        P("vox"),
        P("vox"),
        P("tm", "vox"),
    )
    return jax.shard_map(
        shards,
        mesh=mesh,
        in_specs=placed,
        out_specs=(P(), P("tm", "vox"), P(None, "vox")),
        check_vma=False,
    )
```

profile of v0, /device:TPU:0, one launch (start us, length us, event | category | flops | bytes accessed | tf_op | source)
XLA Modules:
  0.0 259.4 jit_solution(6205240970641587257)
XLA Ops:
  7.2 0.9 slice.434
  8.1 2.3 collective-permute-start
  10.5 0.8 reduce-window.8
  11.3 0.1 convert_reduce_fusion
  11.4 0.7 compare_and_fusion.28
  12.1 0.6 compare_and_fusion.14
  12.7 0.7 compare_and_fusion.15
  13.3 0.7 compare_and_fusion.29
  14.0 0.7 compare_and_fusion.30
  14.7 0.9 convolution_bitcast_fusion.2
  15.5 22.5 %psum.28 = f32[16]{0:T(128)S(1)} all-reduce(f32[16]{0:T(128)S(1)} %convolution_bitcast_fusion.2), channel_id=1, replica_groups=mesh['tm'=4,'vox'=8] {'vox'}, use_global_device_ids=true, to_apply=%region_0.0 | all-reduce | flops 16 | bytes 128 | tf_op jit(solution)/shard_map/psum | solution.py:113
  38.0 0.8 convolution_bitcast_fusion.1
  38.9 0.1 convert_reduce_fusion.2
  39.0 0.7 compare_and_fusion.32
  39.7 0.7 broadcast_multiply_fusion.1
  40.4 0.8 fusion.118
  41.2 1.1 convolution_bitcast_fusion
  42.3 1.5 fusion.119
  47.1 2.5 copy.21
  49.7 1.7 multiply_convert_fusion
  51.5 0.5 fusion.8
  52.0 2.0 fusion.9
  54.0 2.8 %conditional.5 = (bf16[256,128]{1,0:T(8,128)(2,1)S(1)}) conditional(s32[]{:T(128)} %bitcast.5, () %tuple.38, (bf16[1024,640]{0,1:T(8,128)(2,1)S(1)}, bf16[256,1024]{1,0:T(8,128)(2,1)}) %tuple.45), branch_computations={%region_3.4_spmd, %region_4.5_spmd} | conditional | flops 67141632 | bytes 3473416 | solution.py:94
  54.0 1.5 copy.22
  55.5 1.4 convolution_convert_fusion
  56.9 0.6 constant_dynamic-update-slice_fusion.6
  57.5 2.8 %conditional.9 = (bf16[256,128]{1,0:T(8,128)(2,1)S(1)}) conditional(s32[]{:T(128)} %bitcast.16, () %tuple.43, (bf16[1024,640]{0,1:T(8,128)(2,1)S(1)}, bf16[256,1024]{1,0:T(8,128)(2,1)}) %tuple.45), branch_computations={%region_11.12_spmd, %region_12.13_spmd} | conditional | flops 67141632 | bytes 3473416 | solution.py:94
  57.5 1.5 copy.26
  59.0 1.4 convolution_convert_fusion.4
  60.4 3.5 %conditional.8 = (bf16[256,128]{1,0:T(8,128)(2,1)}) conditional(s32[]{:T(128)} %bitcast.15, () %tuple.42, (bf16[1024,640]{0,1:T(8,128)(2,1)S(1)}, bf16[256,1024]{1,0:T(8,128)(2,1)}) %tuple.45), branch_computations={%region_9.10_spmd, %region_10.11_spmd} | conditional | flops 67141632 | bytes 3473416 | solution.py:94
  60.4 1.5 copy.25
  61.9 2.0 convolution_convert_fusion.3
  63.9 3.5 %conditional.7 = (bf16[256,128]{1,0:T(8,128)(2,1)}) conditional(s32[]{:T(128)} %bitcast.14, () %tuple.41, (bf16[1024,640]{0,1:T(8,128)(2,1)S(1)}, bf16[256,1024]{1,0:T(8,128)(2,1)}) %tuple.45), branch_computations={%region_7.8_spmd, %region_8.9_spmd} | conditional | flops 67141632 | bytes 3473416 | solution.py:94
  63.9 1.5 copy.24
  65.3 2.0 convolution_convert_fusion.2
  67.4 3.5 %conditional.6 = (bf16[256,128]{1,0:T(8,128)(2,1)}) conditional(s32[]{:T(128)} %bitcast.13, () %tuple.40, (bf16[1024,640]{0,1:T(8,128)(2,1)S(1)}, bf16[256,1024]{1,0:T(8,128)(2,1)}) %tuple.45), branch_computations={%region_5.6_spmd, %region_6.7_spmd} | conditional | flops 67141632 | bytes 3473416 | solution.py:94
  67.4 1.5 copy.23
  68.8 2.0 convolution_convert_fusion.1
  70.8 1.5 constant_dynamic-update-slice_fusion.5
  72.3 1.5 constant_dynamic-update-slice_fusion.4
  73.8 1.5 constant_dynamic-update-slice_fusion.3
  75.3 0.7 constant_dynamic-update-slice_fusion.2
  76.0 0.7 slice.561
  76.7 1.3 collective-permute-start.1
  78.0 1.3 slice_reduce_fusion.15
  79.3 9.5 %broadcast_multiply_fusion = (f32[256,640]{1,0:T(8,128)S(1)}, f32[256,640]{1,0:T(8,128)}) fusion(f32[640]{0:T(1024)S(1)} %broadcast_multiply_fusion.1, bf16[256,640]{1,0:T(8,128)(2,1)} %param.29, bf16[256,640]{1,0:T(8,128)(2,1)} %constant_dynamic-update-slice_fusion.2, bf16[15,640]{1,0:T(8,128)(2,1)S(1)} %collective-permute-done.1, ...), kind=kLoop, calls=%fused_computation.154 | loop fusion | flops 18186240 | bytes 2032896 | tf_op jit(solution)/shard_map/mul | solution.py:124
  88.9 1.3 collective-permute-start.2
  90.2 0.1 compare_and_fusion.13
  90.3 3.6 %collective-permute-done.2 = f32[15,640]{1,0:T(8,128)S(1)} collective-permute-done((f32[15,640]{1,0:T(8,128)S(1)}, f32[15,640]{1,0:T(8,128)S(1)}, u32[]{:S(2)}, u32[]{:S(2)}) %collective-permute-start.2) | collective-permute-done | bytes 38432 | tf_op jit(solution)/shard_map/ppermute | solution.py:15
  94.0 3.4 %fusion.23 = bf16[256,640]{1,0:T(8,128)(2,1)S(1)} fusion(f32[15,640]{1,0:T(8,128)S(1)} %collective-permute-done.2, f32[256,640]{1,0:T(8,128)S(1)} %get-tuple-element.91, f32[640]{0:T(1024)S(1)} %get-tuple-element.87, f32[640]{0:T(1024)S(1)} %get-tuple-element.88, f32[640]{0:T(1024)S(1)} %get-tuple-element.74, f32[640]{0:T(1024)S(1)} %get-tuple-element.75, ...), kind=kLoop, calls=%fused_computation.65 | loop fusion | flops 10321920 | bytes 1066496 | tf_op jit(solution)/shard_map/convert_element_type | solution.py:138
  97.4 0.7 copy-done.1
  98.2 1.6 fusion.120
  99.8 1.9 mul.406
  101.7 3.3 %copy.27 = f32[1024,640]{1,0:T(8,128)} copy(f32[1024,640]{0,1:T(8,128)} %bitcast.41) | data formatting | bytes 5242880 | tf_op jit(solution)/shard_map/mul | solution.py:84
  104.9 71.6 %all-reduce.3.cloned.1.call-done = f32[256,1024]{1,0:T(8,128)} async-done(((f32[256,1024]{1,0:T(8,128)}), f32[256,1024]{1,0:T(8,128)}) %all-reduce.3.cloned.1.call-update) | async-done | bytes 1048592 | tf_op jit(solution)/shard_map/psum | solution.py:159
  176.5 2.1 fusion.99
  178.8 4.0 %convolution_multiply_fusion = f32[1024,640]{1,0:T(8,128)} fusion(f32[1024,640]{1,0:T(8,128)} %copy.27, bf16[256,1024]{1,0:T(8,128)(2,1)} %get-tuple-element.136, bf16[256,640]{1,0:T(8,128)(2,1)S(1)} %copy-done.2), kind=kOutput, calls=%fused_computation.39 | convolution fusion | flops 336199680 | bytes 6094848 | tf_op jit(solution)/shard_map/dot_general | solution.py:139
  182.9 0.6 copy-done.7
  183.5 0.1 divide_bitcast_fusion
  183.6 0.4 copy-done.3
  183.9 0.8 fusion.17
  184.7 39.8 %psum.29 = f32[]{:T(128)} all-reduce(f32[]{:T(128)} %fusion.17), channel_id=1, replica_groups=mesh['tm'=4,'vox'=8] {'tm','vox'}, use_global_device_ids=true, to_apply=%region_15.16 | all-reduce | flops 1 | bytes 8 | tf_op jit(solution)/shard_map/psum | solution.py:123
  225.2 24.7 %reduce-scatter.2.cloned.1.call-done = f32[256,640]{1,0:T(8,128)} async-done(((f32[1024,640]{1,0:T(8,128)}), f32[256,640]{1,0:T(8,128)}) %reduce-scatter.2.cloned.1.call-update) | async-done | bytes 655376 | tf_op jit(solution)/shard_map/reduce_scatter | solution.py:142
  249.9 1.9 copy.45
  (51 shorter events, 0.4 us)
Async XLA Ops:
  7.2 44.8 %copy-start = (bf16[1024,1024]{1,0:T(8,128)(2,1)S(1)}, bf16[1024,1024]{1,0:T(8,128)(2,1)}, u32[]{:S(2)}) copy-start(bf16[1024,1024]{1,0:T(8,128)(2,1)} %param.22) | copy-start | bytes 6291460
  7.2 169.4 %all-reduce.3.cloned.1.call-start = ((), (), s32[]{:S(2)}) async-start(), calls=%async_computation.2 | async-start | bytes 2097152 | tf_op jit(solution)/shard_map/psum | solution.py:159
  8.1 43.2 %collective-permute-start = (bf16[16,1024]{1,0:T(8,128)(2,1)S(1)}, bf16[16,1024]{1,0:T(8,128)(2,1)S(1)}, u32[]{:S(2)}, u32[]{:S(2)}) collective-permute-start(bf16[16,1024]{1,0:T(8,128)(2,1)S(1)} %slice.434), channel_id=1, source_target_pairs={{0,8},{8,16},{16,24},{1,9},{9,17},{17,25},{2,10},{10,18},{18,26},{... | collective-permute-start | bytes 98312 | tf_op jit(solution)/shard_map/ppermute | solution.py:15
  38.9 0.8 copy-start.18
  49.6 1.7 copy-start.4
  49.6 1.8 copy-start.15
  49.6 1.8 copy-start.16
  49.7 1.8 copy-start.17
  52.0 2.1 copy-start.5
  73.8 20.1 %copy-start.8 = (pred[256]{0:T(512)(128)(4,1)S(1)}, pred[256]{0:T(512)(128)(4,1)}, u32[]{:S(2)}) copy-start(pred[256]{0:T(512)(128)(4,1)} %get-tuple-element.107) | copy-start | bytes 772
  73.8 20.1 %copy-start.9 = (pred[256]{0:T(512)(128)(4,1)S(1)}, pred[256]{0:T(512)(128)(4,1)}, u32[]{:S(2)}) copy-start(pred[256]{0:T(512)(128)(4,1)} %get-tuple-element.96) | copy-start | bytes 772
  73.8 20.1 %copy-start.10 = (pred[256]{0:T(512)(128)(4,1)S(1)}, pred[256]{0:T(512)(128)(4,1)}, u32[]{:S(2)}) copy-start(pred[256]{0:T(512)(128)(4,1)} %get-tuple-element.97) | copy-start | bytes 772
  73.8 20.1 %copy-start.11 = (pred[256]{0:T(512)(128)(4,1)S(1)}, pred[256]{0:T(512)(128)(4,1)}, u32[]{:S(2)}) copy-start(pred[256]{0:T(512)(128)(4,1)} %get-tuple-element.98) | copy-start | bytes 772
  73.8 20.1 %copy-start.12 = (pred[256]{0:T(512)(128)(4,1)S(1)}, pred[256]{0:T(512)(128)(4,1)}, u32[]{:S(2)}) copy-start(pred[256]{0:T(512)(128)(4,1)} %get-tuple-element.99) | copy-start | bytes 772
  73.8 20.1 %copy-start.13 = (pred[256]{0:T(512)(128)(4,1)S(1)}, pred[256]{0:T(512)(128)(4,1)}, u32[]{:S(2)}) copy-start(pred[256]{0:T(512)(128)(4,1)} %get-tuple-element.100) | copy-start | bytes 772
  73.8 20.1 %copy-start.14 = (pred[256]{0:T(512)(128)(4,1)S(1)}, pred[256]{0:T(512)(128)(4,1)}, u32[]{:S(2)}) copy-start(pred[256]{0:T(512)(128)(4,1)} %get-tuple-element.101) | copy-start | bytes 772
  76.7 2.6 %collective-permute-start.1 = (bf16[15,640]{1,0:T(8,128)(2,1)S(1)}, bf16[15,640]{1,0:T(8,128)(2,1)S(1)}, u32[]{:S(2)}, u32[]{:S(2)}) collective-permute-start(bf16[15,640]{1,0:T(8,128)(2,1)S(1)} %slice.561), channel_id=1, source_target_pairs={{0,8},{8,16},{16,24},{1,9},{9,17},{17,25},{2,10},{10,18},{18,26},{... | collective-permute-start | bytes 57608 | tf_op jit(solution)/shard_map/ppermute | solution.py:15
  88.9 5.0 %collective-permute-start.2 = (f32[15,640]{1,0:T(8,128)S(1)}, f32[15,640]{1,0:T(8,128)S(1)}, u32[]{:S(2)}, u32[]{:S(2)}) collective-permute-start(f32[15,640]{1,0:T(8,128)S(1)} %slice.590), channel_id=1, source_target_pairs={{8,0},{16,8},{24,16},{9,1},{17,9},{25,17},{10,2},{18,10},{26,18},{... | collective-permute-start | bytes 115208 | tf_op jit(solution)/shard_map/ppermute | solution.py:15
  97.4 0.8 copy-start.1
  99.7 125.5 %all-reduce.5.cloned.1.call-start = ((), (), s32[]{:S(2)}) async-start(), calls=%async_computation.3 | async-start | bytes 1048576 | tf_op jit(solution)/shard_map/psum | solution.py:165
  101.7 74.9 %copy-start.6 = (bf16[256,1024]{1,0:T(8,128)(2,1)S(1)}, bf16[256,1024]{1,0:T(8,128)(2,1)}, u32[]{:S(2)}) copy-start(bf16[256,1024]{1,0:T(8,128)(2,1)} %copy-done.5) | copy-start | bytes 1572868
  104.9 73.8 %copy-start.2 = (bf16[256,640]{1,0:T(8,128)(2,1)S(1)}, bf16[256,640]{1,0:T(8,128)(2,1)}, u32[]{:S(2)}) copy-start(bf16[256,640]{1,0:T(8,128)(2,1)} %copy-done.1) | copy-start | bytes 983044
  178.7 71.2 %reduce-scatter.2.cloned.1.call-start = ((), (), s32[]{:S(2)}) async-start(), calls=%async_computation.1 | async-start | bytes 3276800 | tf_op jit(solution)/shard_map/reduce_scatter | solution.py:142
  182.8 0.7 copy-start.7
  182.8 0.7 copy-start.19
  182.8 1.1 copy-start.3
Sparse Core Ops, SparseCore 0:
  99.9 76.6 all-reduce.2
  179.0 32.8 all-reduce.4
  215.2 34.6 reduce-scatter.1
where the time goes:
time: 261 us; the launch traced here: 259 us
  waiting for transfers between devices  100 us (38%)
  blocking collectives  62.3 us (24%)
  local copies, waits for them, and re-layouts  29.8 us (11%)
  other arithmetic  21.8 us (8%)
  matrix products  21.4 us (8%)
  between operations  19.2 us (7%)
  starting transfers between devices  5.04 us (2%)
    psum x1, waiting for transfers between devices, shards(): summed_grad = lax.psum(full_grad, 'vox')  71.6 us
    psum x1, blocking collectives, shards(): loss_total = lax.psum(partial_loss, ('tm', 'vox')) / (subjects * total_rows)  39.8 us
    reduce_scatter x1, waiting for transfers between devices, shards(): lax.psum_scatter((raw_rows.reshape(lax.axis_size('tm') * (feature_count /...  24.7 us
    psum x1, blocking collectives, shards(): subject_voxels = lax.psum(local_counts, 'vox')  22.5 us
    unnamed x47, local copies, waits for them, and re-layouts  11.3 us
    mul x2, other arithmetic, shards(): pred_grad = 2.0 * voxel_weight[None, :] * misfit  10.3 us
    dot_general x5, matrix products, live_block(): jnp.dot(operands[0], operands[1], preferred_element_type=jnp.float32)  8.82 us
    another operation x5, local copies, waits for them, and re-layouts  7.27 us
  transfers between devices with their start and end apart: 6, of which 3 were waited for; matrix products, arithmetic and copies ran while one was open for 10% of the time, Pallas kernels for 0%

commit v1 on v0

--- a/solution.py
+++ b/solution.py
@@ -2,6 +2,7 @@
 import jax.numpy as jnp
 from jax import lax
 from jax.sharding import PartitionSpec as P
+from jax.lax import all_gather
 
 BLOCK_VOX = 128
 KERNEL_TAPS = 3
@@ -156,7 +157,7 @@
     full_grad = lax.dot_general(
         response_half, effective, (((1,), (1,)), ((), ())), preferred_element_type=jnp.float32
     )
-    summed_grad = lax.psum(full_grad, "vox")
+    summed_grad = all_gather(full_grad, axis_name="vox").sum(axis=0)
     grad_cols = lax.dynamic_slice_in_dim(summed_grad, col_start, share_width, 1)
     pre_grad = jax.vjp(jax.nn.gelu, pre_cols)[1](grad_cols)[0].astype(jnp.bfloat16)
     point_part = lax.dot_general(

time: 261 us -> 279 us (1.069)
  waiting for transfers between devices: 100 us -> 118 us
  other arithmetic: 21.8 us -> 27.5 us
  local copies, waits for them, and re-layouts: 29.8 us -> 26.2 us
    all_gather x0 -> x1, waiting for transfers between devices: none -> 114 us  [shards(): summed_grad = all_gather(full_grad, axis_name='vox').sum(axis=0)]
    psum x1 -> x0, waiting for transfers between devices: 71.6 us -> none  [shards(): summed_grad = lax.psum(full_grad, 'vox')]
    reduce_scatter x1, waiting for transfers between devices: 24.7 us -> 0.03 us  [shards(): lax.psum_scatter((raw_rows.reshape(lax.axis_size('tm') * (feature_count /...]
    reduce_sum x0 -> x1, other arithmetic: none -> 5.49 us  [shards(): summed_grad = all_gather(full_grad, axis_name='vox').sum(axis=0)]
    unnamed x47 -> x49, local copies, waits for them, and re-layouts: 11.3 us -> 7.74 us
  transfers between devices with their start and end apart: 6 -> 6, of which waited for: 3 -> 2; matrix products, arithmetic and copies ran while one was open for 10% -> 12% of each run, Pallas kernels for 0% -> 0%
where the time goes in v1:
time: 279 us; the launch traced here: 278 us
  waiting for transfers between devices  118 us (42%)
  blocking collectives  61.1 us (22%)
  other arithmetic  27.5 us (10%)
  local copies, waits for them, and re-layouts  26.2 us (9%)
  between operations  20.8 us (7%)
  matrix products  19.8 us (7%)
  starting transfers between devices  5.04 us (2%)
    all_gather x1, waiting for transfers between devices, shards(): summed_grad = all_gather(full_grad, axis_name='vox').sum(axis=0)  114 us
    psum x1, blocking collectives, shards(): loss_total = lax.psum(partial_loss, ('tm', 'vox')) / (subjects * total_rows)  38.6 us
    psum x1, blocking collectives, shards(): subject_voxels = lax.psum(local_counts, 'vox')  22.5 us
    mul x2, other arithmetic, shards(): pred_grad = 2.0 * voxel_weight[None, :] * misfit  10.4 us
    unnamed x49, local copies, waits for them, and re-layouts  7.74 us
    another operation x5, local copies, waits for them, and re-layouts  7.26 us
    dot_general x5, matrix products, live_block(): jnp.dot(operands[0], operands[1], preferred_element_type=jnp.float32)  6.96 us
  transfers between devices with their start and end apart: 6, of which 2 were waited for; matrix products, arithmetic and copies ran while one was open for 12% of the time, Pallas kernels for 0%

profile of v1, /device:TPU:0, one launch (start us, length us, event | category | flops | bytes accessed | tf_op | source)
XLA Modules:
  0.0 278.2 jit_solution(8788514093957331023)
XLA Ops:
  8.1 0.9 slice.434
  9.0 2.3 collective-permute-start
  11.3 0.8 reduce-window.8
  12.2 0.1 convert_reduce_fusion
  12.3 0.7 compare_and_fusion.30
  12.9 0.7 compare_and_fusion.29
  13.6 0.7 compare_and_fusion.15
  14.3 0.7 compare_and_fusion.14
  15.0 0.9 convolution_bitcast_fusion.2
  15.8 0.7 compare_and_fusion.28
  16.5 22.5 %psum.21 = f32[16]{0:T(128)S(1)} all-reduce(f32[16]{0:T(128)S(1)} %convolution_bitcast_fusion.2), channel_id=1, replica_groups=mesh['tm'=4,'vox'=8] {'vox'}, use_global_device_ids=true, to_apply=%region_0.0 | all-reduce | flops 16 | bytes 128 | tf_op jit(solution)/shard_map/psum | solution.py:114
  39.0 0.8 convolution_bitcast_fusion.1
  39.8 0.7 broadcast_multiply_fusion.1
  40.6 1.1 convolution_bitcast_fusion
  41.6 0.8 fusion.118
  42.5 0.1 convert_reduce_fusion.2
  42.6 0.7 compare_and_fusion.32
  43.3 1.4 fusion.119
  45.3 2.5 copy.21
  50.4 1.7 multiply_convert_fusion
  52.2 0.5 fusion.8
  52.7 2.0 fusion.9
  54.8 2.8 %conditional.5 = (bf16[256,128]{1,0:T(8,128)(2,1)S(1)}) conditional(s32[]{:T(128)} %bitcast.5, () %tuple.38, (bf16[1024,640]{0,1:T(8,128)(2,1)S(1)}, bf16[256,1024]{1,0:T(8,128)(2,1)}) %tuple.45), branch_computations={%region_3.4_spmd, %region_4.5_spmd} | conditional | flops 67141632 | bytes 3473416 | solution.py:95
  54.8 1.5 copy.22
  56.2 1.4 convolution_convert_fusion
  57.6 0.6 constant_dynamic-update-slice_fusion.6
  58.2 2.8 %conditional.6 = (bf16[256,128]{1,0:T(8,128)(2,1)S(1)}) conditional(s32[]{:T(128)} %bitcast.13, () %tuple.40, (bf16[1024,640]{0,1:T(8,128)(2,1)S(1)}, bf16[256,1024]{1,0:T(8,128)(2,1)}) %tuple.45), branch_computations={%region_5.6_spmd, %region_6.7_spmd} | conditional | flops 67141632 | bytes 3473416 | solution.py:95
  58.3 1.5 copy.23
  59.7 1.4 convolution_convert_fusion.1
  61.1 0.6 constant_dynamic-update-slice_fusion.5
  61.7 2.8 %conditional.7 = (bf16[256,128]{1,0:T(8,128)(2,1)S(1)}) conditional(s32[]{:T(128)} %bitcast.14, () %tuple.41, (bf16[1024,640]{0,1:T(8,128)(2,1)S(1)}, bf16[256,1024]{1,0:T(8,128)(2,1)}) %tuple.45), branch_computations={%region_7.8_spmd, %region_8.9_spmd} | conditional | flops 67141632 | bytes 3473416 | solution.py:95
  61.7 1.5 copy.24
  63.2 1.4 convolution_convert_fusion.2
  64.6 0.6 constant_dynamic-update-slice_fusion.4
  65.2 2.8 %conditional.8 = (bf16[256,128]{1,0:T(8,128)(2,1)S(1)}) conditional(s32[]{:T(128)} %bitcast.15, () %tuple.42, (bf16[1024,640]{0,1:T(8,128)(2,1)S(1)}, bf16[256,1024]{1,0:T(8,128)(2,1)}) %tuple.45), branch_computations={%region_9.10_spmd, %region_10.11_spmd} | conditional | flops 67141632 | bytes 3473416 | solution.py:95
  65.2 1.5 copy.25
  66.7 1.4 convolution_convert_fusion.3
  68.1 0.6 constant_dynamic-update-slice_fusion.3
  68.7 2.8 %conditional.9 = (bf16[256,128]{1,0:T(8,128)(2,1)S(1)}) conditional(s32[]{:T(128)} %bitcast.16, () %tuple.43, (bf16[1024,640]{0,1:T(8,128)(2,1)S(1)}, bf16[256,1024]{1,0:T(8,128)(2,1)}) %tuple.45), branch_computations={%region_11.12_spmd, %region_12.13_spmd} | conditional | flops 67141632 | bytes 3473416 | solution.py:95
  68.7 1.5 copy.26
  70.2 1.4 convolution_convert_fusion.4
  71.6 0.6 constant_dynamic-update-slice_fusion.2
  72.3 0.7 slice.561
  73.0 1.3 collective-permute-start.1
  74.3 1.3 slice_reduce_fusion.15
  75.7 9.7 %broadcast_multiply_fusion = (f32[256,640]{1,0:T(8,128)S(1)}, f32[256,640]{1,0:T(8,128)}) fusion(f32[640]{0:T(1024)S(1)} %broadcast_multiply_fusion.1, bf16[256,640]{1,0:T(8,128)(2,1)} %param.29, bf16[256,640]{1,0:T(8,128)(2,1)} %constant_dynamic-update-slice_fusion.2, bf16[15,640]{1,0:T(8,128)(2,1)S(1)} %collective-permute-done.1, ...), kind=kLoop, calls=%fused_computation.154 | loop fusion | flops 18186240 | bytes 2032896 | tf_op jit(solution)/shard_map/mul | solution.py:125
  85.4 1.3 collective-permute-start.2
  86.7 0.1 compare_and_fusion.13
  86.7 3.6 %collective-permute-done.2 = f32[15,640]{1,0:T(8,128)S(1)} collective-permute-done((f32[15,640]{1,0:T(8,128)S(1)}, f32[15,640]{1,0:T(8,128)S(1)}, u32[]{:S(2)}, u32[]{:S(2)}) %collective-permute-start.2) | collective-permute-done | bytes 38432 | tf_op jit(solution)/shard_map/ppermute | solution.py:16
  90.4 3.4 %fusion.23 = bf16[256,640]{1,0:T(8,128)(2,1)S(1)} fusion(f32[15,640]{1,0:T(8,128)S(1)} %collective-permute-done.2, f32[256,640]{1,0:T(8,128)S(1)} %get-tuple-element.91, f32[640]{0:T(1024)S(1)} %get-tuple-element.87, f32[640]{0:T(1024)S(1)} %get-tuple-element.88, f32[640]{0:T(1024)S(1)} %get-tuple-element.74, f32[640]{0:T(1024)S(1)} %get-tuple-element.75, ...), kind=kLoop, calls=%fused_computation.65 | loop fusion | flops 10321920 | bytes 1066496 | tf_op jit(solution)/shard_map/convert_element_type | solution.py:139
  93.9 0.7 copy-done.1
  94.6 1.6 fusion.120
  96.2 0.0 reduce-scatter.2.cloned.1.call-start
  96.2 1.9 mul.406
  98.1 3.4 %copy.27 = f32[1024,640]{1,0:T(8,128)} copy(f32[1024,640]{0,1:T(8,128)} %bitcast.42) | data formatting | bytes 5242880 | tf_op jit(solution)/shard_map/mul | solution.py:85
  101.5 4.3 %convolution_multiply_fusion = f32[1024,640]{1,0:T(8,128)} fusion(f32[1024,640]{1,0:T(8,128)} %copy.27, bf16[256,1024]{1,0:T(8,128)(2,1)S(1)} %copy-done.7, bf16[256,640]{1,0:T(8,128)(2,1)S(1)} %copy-done.2), kind=kOutput, calls=%fused_computation.39 | convolution fusion | flops 336199680 | bytes 6094848 | tf_op jit(solution)/shard_map/dot_general | solution.py:140
  105.9 0.0 all-reduce.2.cloned.1.call-start
  105.9 113.9 %all-gather.3.cloned.1.call-done = f32[2048,1024]{1,0:T(8,128)} async-done(((f32[256,1024]{1,0:T(8,128)}), f32[2048,1024]{1,0:T(8,128)}) %all-gather.3.cloned.1.call-update) | async-done | bytes 8388624 | tf_op jit(solution)/shard_map/all_gather | solution.py:160
  219.8 5.5 %reduce_sum.49 = f32[256,1024]{1,0:T(8,128)} reduce(f32[8,256,1024]{2,1,0:T(8,128)} %bitcast.43, f32[]{:T(128)} %constant.25.clone.1), dimensions={0}, to_apply=%region_18.19 | reduce | flops 1835008 | bytes 9437188 | tf_op jit(solution)/shard_map/reduce_sum | solution.py:160
  225.3 2.2 fusion.99
  227.6 0.1 divide_bitcast_fusion
  227.6 0.8 fusion.17
  228.4 38.6 %psum.22 = f32[]{:T(128)} all-reduce(f32[]{:T(128)} %fusion.17), channel_id=1, replica_groups=mesh['tm'=4,'vox'=8] {'tm','vox'}, use_global_device_ids=true, to_apply=%region_15.16 | all-reduce | flops 1 | bytes 8 | tf_op jit(solution)/shard_map/psum | solution.py:124
  267.8 1.9 copy.44
  (54 shorter events, 0.3 us)
Async XLA Ops:
  8.0 44.7 %copy-start = (bf16[1024,1024]{1,0:T(8,128)(2,1)S(1)}, bf16[1024,1024]{1,0:T(8,128)(2,1)}, u32[]{:S(2)}) copy-start(bf16[1024,1024]{1,0:T(8,128)(2,1)} %param.22) | copy-start | bytes 6291460
  8.0 211.8 %all-gather.3.cloned.1.call-start = ((), (), s32[]{:S(2)}) async-start(), calls=%async_computation.3 | async-start | bytes 9437184 | tf_op jit(solution)/shard_map/all_gather | solution.py:160
  9.0 43.1 %collective-permute-start = (bf16[16,1024]{1,0:T(8,128)(2,1)S(1)}, bf16[16,1024]{1,0:T(8,128)(2,1)S(1)}, u32[]{:S(2)}, u32[]{:S(2)}) collective-permute-start(bf16[16,1024]{1,0:T(8,128)(2,1)S(1)} %slice.434), channel_id=1, source_target_pairs={{0,8},{8,16},{16,24},{1,9},{9,17},{17,25},{2,10},{10,18},{18,26},{... | collective-permute-start | bytes 98312 | tf_op jit(solution)/shard_map/ppermute | solution.py:16
  39.8 0.7 copy-start.19
  50.3 1.8 copy-start.4
  50.4 1.8 copy-start.16
  50.4 1.8 copy-start.17
  50.4 1.8 copy-start.18
  52.7 2.1 copy-start.5
  71.6 18.8 %copy-start.9 = (pred[256]{0:T(512)(128)(4,1)S(1)}, pred[256]{0:T(512)(128)(4,1)}, u32[]{:S(2)}) copy-start(pred[256]{0:T(512)(128)(4,1)} %get-tuple-element.101) | copy-start | bytes 772
  71.6 18.8 %copy-start.10 = (pred[256]{0:T(512)(128)(4,1)S(1)}, pred[256]{0:T(512)(128)(4,1)}, u32[]{:S(2)}) copy-start(pred[256]{0:T(512)(128)(4,1)} %get-tuple-element.102) | copy-start | bytes 772
  71.6 18.8 %copy-start.11 = (pred[256]{0:T(512)(128)(4,1)S(1)}, pred[256]{0:T(512)(128)(4,1)}, u32[]{:S(2)}) copy-start(pred[256]{0:T(512)(128)(4,1)} %get-tuple-element.103) | copy-start | bytes 772
  71.6 18.8 %copy-start.12 = (pred[256]{0:T(512)(128)(4,1)S(1)}, pred[256]{0:T(512)(128)(4,1)}, u32[]{:S(2)}) copy-start(pred[256]{0:T(512)(128)(4,1)} %get-tuple-element.104) | copy-start | bytes 772
  71.6 18.8 %copy-start.13 = (pred[256]{0:T(512)(128)(4,1)S(1)}, pred[256]{0:T(512)(128)(4,1)}, u32[]{:S(2)}) copy-start(pred[256]{0:T(512)(128)(4,1)} %get-tuple-element.105) | copy-start | bytes 772
  71.6 18.8 %copy-start.14 = (pred[256]{0:T(512)(128)(4,1)S(1)}, pred[256]{0:T(512)(128)(4,1)}, u32[]{:S(2)}) copy-start(pred[256]{0:T(512)(128)(4,1)} %get-tuple-element.106) | copy-start | bytes 772
  71.6 18.8 %copy-start.15 = (pred[256]{0:T(512)(128)(4,1)S(1)}, pred[256]{0:T(512)(128)(4,1)}, u32[]{:S(2)}) copy-start(pred[256]{0:T(512)(128)(4,1)} %get-tuple-element.107) | copy-start | bytes 772
  73.0 2.6 collective-permute-start.1
  85.4 5.0 %collective-permute-start.2 = (f32[15,640]{1,0:T(8,128)S(1)}, f32[15,640]{1,0:T(8,128)S(1)}, u32[]{:S(2)}, u32[]{:S(2)}) collective-permute-start(f32[15,640]{1,0:T(8,128)S(1)} %slice.590), channel_id=1, source_target_pairs={{8,0},{16,8},{24,16},{9,1},{17,9},{25,17},{10,2},{18,10},{26,18},{... | collective-permute-start | bytes 115208 | tf_op jit(solution)/shard_map/ppermute | solution.py:16
  93.9 0.7 copy-start.1
  96.2 171.5 %reduce-scatter.2.cloned.1.call-start = ((), (), s32[]{:S(2)}) async-start(), calls=%async_computation.1 | async-start | bytes 3276800 | tf_op jit(solution)/shard_map/reduce_scatter | solution.py:143
  98.1 3.4 %copy-start.2 = (bf16[256,640]{1,0:T(8,128)(2,1)S(1)}, bf16[256,640]{1,0:T(8,128)(2,1)}, u32[]{:S(2)}) copy-start(bf16[256,640]{1,0:T(8,128)(2,1)} %copy-done.1) | copy-start | bytes 983044
  98.1 3.4 %copy-start.7 = (bf16[256,1024]{1,0:T(8,128)(2,1)S(1)}, bf16[256,1024]{1,0:T(8,128)(2,1)}, u32[]{:S(2)}) copy-start(bf16[256,1024]{1,0:T(8,128)(2,1)} %get-tuple-element.136) | copy-start | bytes 1572868
  105.9 161.9 %all-reduce.2.cloned.1.call-start = ((), (), s32[]{:S(2)}) async-start(), calls=%async_computation.2 | async-start | bytes 1048576 | tf_op jit(solution)/shard_map/psum | solution.py:166
  219.8 5.5 %copy-start.6 = (bf16[256,1024]{1,0:T(8,128)(2,1)S(1)}, bf16[256,1024]{1,0:T(8,128)(2,1)}, u32[]{:S(2)}) copy-start(bf16[256,1024]{1,0:T(8,128)(2,1)} %copy-done.5) | copy-start | bytes 1572868
  225.3 2.3 copy-start.8
  225.3 2.3 copy-start.20
  225.3 2.4 copy-start.3
Sparse Core Ops, SparseCore 0:
  96.3 123.4 all-gather.2
Sparse Core Ops, SparseCore 1:
  105.9 33.1 reduce-scatter.1
  227.6 31.4 all-reduce.1
